TPU v7x, 256 devices: a whole 4x4x8 slice. The times are simulated.
256 devices in a mesh: lat: 32 (over z, y_hi, core), lon: 8 (over y_lo, x).
Axes of the slice: x: 4, y: 4 (y_hi: 2, y_lo: 2; y = y_hi * 2 + y_lo), z: 8, core: 2. Of those that a mesh axis runs over, the one named last changes fastest.
Arguments:
- state_field: bfloat16 [73, 256, 1024], P(None, 'lat', 'lon'), may hold values from -6 to 6
- support_rows: int32 [128, 5], P('lat'), may hold values from -2 to 2, as said below
- window_bands: int32 [32], replicated, may hold values from 0 to 127, as said below
- conv_weight: bfloat16 [5, 3, 73, 256], replicated, may hold values from -0.1875 to 0.1875
- w_query: bfloat16 [256, 256], replicated
- w_key: bfloat16 [256, 256], replicated
- w_value: bfloat16 [256, 256], replicated, may hold values from -0.375 to 0.375
- w_out: bfloat16 [256, 256], replicated, may hold values from -0.75 to 0.75
Outputs:
- window_out: bfloat16 [32, 512, 256], P('lat', 'lon')
Inputs may be any that keep to these rules, and one draw needn't show every extreme that they name: `support_rows`: each row is a permutation of the 5 offsets from -2 to 2. `window_bands`: 32 distinct token bands.
All inputs are finite; a program needn't handle non-finite values.
Results may differ from a plain program's by a relative error of at most 0.019.
Values may be sent and summed in bfloat16 or wider, within the bound.
A program may use at most 64 MiB of HBM per device.

v0:
```python
import math
import jax
import jax.numpy as jnp
from jax import lax
from jax.sharding import PartitionSpec as P

D = 256
H = 4


def padded(x, sides, width):
    for axis, dim in sides:
        devices, length = (lax.axis_size(axis), x.shape[dim])
        up = [(i, (i + 1) % devices) for i in range(devices - 1)]
        down = [(j, i) for i, j in up]
        last = lax.slice_in_dim(x, length - width, length, axis=dim)
        leading = lax.slice_in_dim(x, 0, width, axis=dim)
        before = lax.ppermute(last, axis, up)
        after = lax.ppermute(leading, axis, down)
        x = jnp.concatenate([before, x, after], axis=dim)
    return x


def shifted(x, axis, by):
    devices = lax.axis_size(axis)
    return lax.ppermute(x, axis, [(i, (i + by) % devices) for i in range(devices)])


def conv_features(extended, support_rows, conv_weight):
    bands = support_rows.shape[0]
    width = (extended.shape[2] - 1) // 2
    row_index = 2 * jnp.arange(bands, dtype=jnp.int32)[:, None] + support_rows + 2
    picked = jnp.take(extended, row_index, axis=1)
    tapped = jnp.stack(
        [picked[..., column_tap : column_tap + 2 * width : 2] for column_tap in range(3)], axis=3
    )
    patches = jnp.transpose(tapped, (1, 4, 2, 3, 0)).reshape(bands * width, -1)
    raw = jnp.dot(
        patches, conv_weight.reshape(-1, conv_weight.shape[-1]), preferred_element_type=jnp.float32
    )
    factor = lax.rsqrt(jnp.mean(raw * raw, axis=-1, keepdims=True) + 1e-06)
    return (raw * factor).astype(jnp.bfloat16).reshape(bands, width, -1)


def absorb(carry, block_keys, block_values, block_area, queries, scale):
    running_max, running_sum, mixed = carry
    scores = (
        jnp.einsum("qhd,khd->qhk", queries, block_keys, preferred_element_type=jnp.float32) * scale
        + block_area
    )
    new_max = jnp.maximum(running_max, jnp.max(scores, axis=-1))
    factor = jnp.exp(running_max - new_max)
    weights = jnp.exp(scores - new_max[..., None])
    running_sum = running_sum * factor + jnp.sum(weights, axis=-1)
    update = jnp.einsum(
        "qhk,khd->qhd",
        weights.astype(jnp.bfloat16),
        block_values,
        preferred_element_type=jnp.float32,
    )
    mixed = mixed * factor[..., None] + update
    return (new_max, running_sum, mixed)


def sweep(carry, keys, values, queries, band_total):
    rows = keys.shape[0]
    lon_tile = keys.shape[1]
    head_size = D // H
    band_block = math.gcd(rows, max(1, 512 // lon_tile))
    blocks = rows // band_block
    block_len = band_block * lon_tile
    keys_blocks = keys.reshape(blocks, block_len, H, head_size)
    values_blocks = values.reshape(blocks, block_len, H, head_size)
    band_index = jnp.arange(rows, dtype=jnp.int32).astype(jnp.float32)
    centre = (band_index + 0.5) * (math.pi / band_total) - math.pi / 2
    area_rows = jnp.repeat(jnp.log(jnp.cos(centre)), lon_tile).reshape(blocks, block_len)
    scale = 1.0 / math.sqrt(head_size)

    def step_block(state, inputs):
        return (absorb(state, inputs[0], inputs[1], inputs[2], queries, scale), None)

    result, unused = lax.scan(step_block, carry, (keys_blocks, values_blocks, area_rows))
    return result


def per_device(
    state_field, support_rows, window_bands, conv_weight, w_query, w_key, w_value, w_out
):
    lat_tile = support_rows.shape[0]
    lon_tile = state_field.shape[2] // 2
    whole_lon = lon_tile * lax.axis_size("lon")
    band_total = lat_tile * lax.axis_size("lat")
    head_size = D // H
    extended = padded(state_field, (("lat", 1),), 2)
    western = shifted(extended[:, :, -1:], "lon", 1)
    extended = jnp.concatenate([western, extended], axis=2)
    features = conv_features(extended, support_rows, conv_weight)
    flat = features.reshape(-1, D)
    slot_count = window_bands.shape[0] // lax.axis_size("lat")
    local_queries = jnp.dot(flat, w_query, preferred_element_type=jnp.float32).astype(jnp.bfloat16)
    local_queries = local_queries.reshape(lat_tile, lon_tile * D)
    first_band = lax.axis_index("lat") * lat_tile
    wanted = window_bands - first_band
    onehot = (wanted[:, None] == jnp.arange(lat_tile, dtype=jnp.int32)[None, :]).astype(
        jnp.bfloat16
    )
    picked = jnp.dot(onehot, local_queries, preferred_element_type=jnp.float32)
    picked = picked.astype(jnp.bfloat16).astype(jnp.float32)
    mine = lax.psum_scatter(
        picked.reshape(slot_count * lax.axis_size("lat"), lon_tile, D).astype(jnp.bfloat16),
        "lat",
        scatter_dimension=0,
        tiled=True,
    )
    gathered = lax.all_gather(mine, "lon", axis=1, tiled=True)
    query_count = slot_count * whole_lon
    queries = gathered.reshape(query_count, H, head_size)
    initial = (
        jnp.full((query_count, H), -1e30, jnp.float32),
        jnp.zeros((query_count, H), jnp.float32),
        jnp.zeros((query_count, H, head_size), jnp.float32),
    )
    keys_local = (
        jnp.dot(flat, w_key, preferred_element_type=jnp.float32)
        .astype(jnp.bfloat16)
        .reshape(lat_tile, lon_tile, D)
    )
    values_local = (
        jnp.dot(flat, w_value, preferred_element_type=jnp.float32)
        .astype(jnp.bfloat16)
        .reshape(lat_tile, lon_tile, D)
    )
    carry = sweep(
        initial,
        lax.all_gather(keys_local, "lat", axis=0, tiled=True),
        lax.all_gather(values_local, "lat", axis=0, tiled=True),
        queries,
        band_total,
    )
    running_max, running_sum, mixed = carry
    best = lax.pmax(running_max, "lon")
    factor = jnp.exp(running_max - best)
    scaled_mix = (mixed * factor[..., None]).reshape(slot_count, whole_lon, D)
    scaled_sum = (running_sum * factor).reshape(slot_count, whole_lon, H)
    mix_share, sum_share = (
        lax.psum_scatter(
            scaled_mix.astype(jnp.bfloat16), "lon", scatter_dimension=1, tiled=True
        ).astype(jnp.float32),
        lax.psum_scatter(
            scaled_sum.astype(jnp.bfloat16), "lon", scatter_dimension=1, tiled=True
        ).astype(jnp.float32),
    )
    attended = mix_share.reshape(slot_count, lon_tile, H, head_size) / sum_share[..., None]
    attended = attended.astype(jnp.bfloat16).reshape(slot_count * lon_tile, D)
    result = jnp.dot(attended, w_out, preferred_element_type=jnp.float32).astype(jnp.bfloat16)
    return result.reshape(slot_count, lon_tile, D)


def solution(mesh):
    return jax.shard_map(
        per_device,
        mesh=mesh,
        in_specs=(P(None, "lat", "lon"), P("lat", None), P(), P(), P(), P(), P(), P()),
        out_specs=P("lat", "lon", None),
        check_vma=False,
    )
```

profile of v0, /device:TPU:32, one launch (start us, length us, event | category | flops | bytes accessed | tf_op | source)
XLA Modules:
  0.0 605.1 jit_solution(1551652999318973012)
XLA Ops:
  9.7 6.0 collective-permute-start.1
  35.6 114.5 %reduce-scatter.8.cloned.1.call-done = bf16[1,64,256]{2,1,0:T(8,128)(2,1)} async-done(((bf16[32,64,256]{2,1,0:T(8,128)(2,1)}), bf16[1,64,256]{2,1,0:T(8,128)(2,1)}) %reduce-scatter.8.cloned.1.call-update) | async-done | bytes 32784 | tf_op jit(solution)/shard_map/reduce_scatter | solution.py:109
  150.1 28.8 %all_gather.10 = bf16[1,512,256]{2,1,0:T(8,128)(2,1)S(1)} all-gather(bf16[1,64,256]{2,1,0:T(8,128)(2,1)} %reduce-scatter.8.cloned.1.call-done), channel_id=1, replica_groups=mesh['lat'=32,'lon'=8] {'lon'}, dimensions={1}, use_global_device_ids=true | all-gather | bytes 294912 | tf_op jit(solution)/shard_map/all_gather | solution.py:115
  179.0 59.0 %all-gather.3.cloned.1.call-done = bf16[128,64,256]{2,1,0:T(8,128)(2,1)} async-done(((bf16[4,64,256]{2,1,0:T(8,128)(2,1)}), bf16[128,64,256]{2,1,0:T(8,128)(2,1)}) %all-gather.3.cloned.1.call-update) | async-done | bytes 4194320 | tf_op jit(solution)/shard_map/all_gather | solution.py:135
  238.1 12.9 %reshape.113 = bf16[16,512,4,64]{3,2,1,0:T(4,128)(2,1)} reshape(bf16[128,64,256]{2,1,0:T(8,128)(2,1)} %all-gather.3.cloned.1.call-done) | data formatting | bytes 8388608 | tf_op jit(solution)/shard_map/reshape | solution.py:72
  251.0 12.7 %copy.29 = bf16[16,512,4,64]{1,3,2,0:T(8,128)(2,1)} copy(bf16[16,512,4,64]{3,2,1,0:T(4,128)(2,1)} %reshape.113) | data formatting | bytes 8388608
  263.7 60.5 %all-gather.5.cloned.1.call-done = bf16[128,64,256]{2,1,0:T(8,128)(2,1)} async-done(((bf16[4,64,256]{2,1,0:T(8,128)(2,1)}), bf16[128,64,256]{2,1,0:T(8,128)(2,1)}) %all-gather.5.cloned.1.call-update) | async-done | bytes 4194320 | tf_op jit(solution)/shard_map/all_gather | solution.py:136
  324.2 12.9 %reshape.114 = bf16[16,512,4,64]{3,2,1,0:T(4,128)(2,1)} reshape(bf16[128,64,256]{2,1,0:T(8,128)(2,1)} %all-gather.5.cloned.1.call-done) | data formatting | bytes 8388608 | tf_op jit(solution)/shard_map/reshape | solution.py:73
  337.1 12.7 %copy.30 = bf16[16,512,4,64]{1,3,2,0:T(8,128)(2,1)} copy(bf16[16,512,4,64]{3,2,1,0:T(4,128)(2,1)} %reshape.114) | data formatting | bytes 8388608
  349.8 150.0 %while.15 = (s32[]{:T(128)}, f32[512,4]{0,1:T(4,128)S(1)}, f32[512,4]{0,1:T(4,128)S(1)}, f32[512,4,64]{0,2,1:T(8,128)S(1)}, bf16[16,512,4,64]{1,3,2,0:T(8,128)(2...) while((s32[]{:T(128)}, f32[512,4]{0,1:T(4,128)S(1)}, ...), condition=%wide.region_5.6_spmd.clone, body=%wide.region_2.0_spmd.clone.sunk | while | flops 280373248 | bytes 31337616 | solution.py:82
  349.8 3.8 bitcast_reduce_fusion.2
  359.2 3.8 bitcast_reduce_fusion.2
  368.6 3.8 bitcast_reduce_fusion.2
  372.4 3.2 fusion.46
  378.0 3.8 bitcast_reduce_fusion.2
  387.3 3.8 bitcast_reduce_fusion.2
  391.1 3.2 fusion.46
  396.7 3.8 bitcast_reduce_fusion.2
  400.5 3.2 fusion.46
  406.1 3.8 bitcast_reduce_fusion.2
  415.5 3.8 bitcast_reduce_fusion.2
  424.8 3.8 bitcast_reduce_fusion.2
  434.2 3.8 bitcast_reduce_fusion.2
  443.6 3.8 bitcast_reduce_fusion.2
  452.9 3.8 bitcast_reduce_fusion.2
  462.3 3.8 bitcast_reduce_fusion.2
  471.7 3.8 bitcast_reduce_fusion.2
  481.1 3.8 bitcast_reduce_fusion.2
  490.4 3.8 bitcast_reduce_fusion.2
  499.8 18.9 %pmax.7 = f32[512,4]{0,1:T(4,128)S(1)} all-reduce(f32[512,4]{0,1:T(4,128)S(1)} %get-tuple-element.50), channel_id=1, replica_groups=mesh['lat'=32,'lon'=8] {'lon'}, use_global_device_ids=true, to_apply=%region_6.7 | all-reduce | flops 2048 | bytes 16384 | tf_op jit(solution)/shard_map/pmax | solution.py:141
  520.9 34.4 %reduce-scatter.12.cloned.1.call-done = bf16[64,4]{1,0:T(8,128)(2,1)} async-done(((bf16[512,4]{1,0:T(8,128)(2,1)}), bf16[64,4]{1,0:T(8,128)(2,1)}) %reduce-scatter.12.cloned.1.call-update) | async-done | bytes 528
  556.2 40.6 %reduce-scatter.10.cloned.1.call-done = bf16[64,256]{1,0:T(8,128)(2,1)} async-done(((bf16[512,256]{1,0:T(8,128)(2,1)}), bf16[64,256]{1,0:T(8,128)(2,1)}) %reduce-scatter.10.cloned.1.call-update) | async-done | bytes 32784
  (195 shorter events, 106.3 us)
Async XLA Ops:
  6.5 24.8 %copy-start = (bf16[256,256]{1,0:T(8,128)(2,1)S(1)}, bf16[256,256]{1,0:T(8,128)(2,1)}, u32[]{:S(2)}) copy-start(bf16[256,256]{1,0:T(8,128)(2,1)} %param.14) | copy-start | bytes 393220
  6.5 143.6 %reduce-scatter.8.cloned.1.call-start = ((), (), s32[]{:S(2)}) async-start(), calls=%async_computation.4 | async-start | bytes 1081344 | tf_op jit(solution)/shard_map/reduce_scatter | solution.py:109
  7.7 9.5 %collective-permute-start = (bf16[73,2,128]{0,2,1:T(8,128)(2,1)S(1)}, bf16[73,2,128]{0,2,1:T(8,128)(2,1)S(1)}, u32[]{:S(2)}, u32[]{:S(2)}) collective-permute-start(bf16[73,2,128]{0,2,1:T(8,128)(2,1)S(1)} %get-tuple-element.119), channel_id=1, source_target_pairs={{0,8},{8,16},{16,24},{24,32},{32,40},{40,48},{48,56},{56,64},{64,7... | collective-permute-start | bytes 112136 | tf_op jit(solution)/shard_map/ppermute | solution.py:18
  9.7 7.9 %collective-permute-start.1 = (bf16[73,2,128]{0,2,1:T(8,128)(2,1)S(1)}, bf16[73,2,128]{0,2,1:T(8,128)(2,1)S(1)}, u32[]{:S(2)}, u32[]{:S(2)}) collective-permute-start(bf16[73,2,128]{0,2,1:T(8,128)(2,1)S(1)} %get-tuple-element.120), channel_id=1, source_target_pairs={{8,0},{16,8},{24,16},{32,24},{40,32},{48,40},{56,48},{64,56},{72,6... | collective-permute-start | bytes 112136 | tf_op jit(solution)/shard_map/ppermute | solution.py:19
  17.6 5.8 collective-permute-start.2
  29.7 3.7 copy-start.2
  29.8 4.7 copy-start.3
  33.4 204.7 %all-gather.3.cloned.1.call-start = ((), (), s32[]{:S(2)}) async-start(), calls=%async_computation.3 | async-start | bytes 4325376 | tf_op jit(solution)/shard_map/all_gather | solution.py:135
  34.4 289.8 %all-gather.5.cloned.1.call-start = ((), (), s32[]{:S(2)}) async-start(), calls=%async_computation.5 | async-start | bytes 4325376 | tf_op jit(solution)/shard_map/all_gather | solution.py:136
  35.3 520.0 %reduce-scatter.12.cloned.1.call-start = ((), (), s32[]{:S(2)}) async-start(), calls=%async_computation.7 | async-start | bytes 147456
  349.8 247.9 %copy-start.4 = (bf16[256,256]{1,0:T(8,128)(2,1)S(1)}, bf16[256,256]{1,0:T(8,128)(2,1)}, u32[]{:S(2)}) copy-start(bf16[256,256]{1,0:T(8,128)(2,1)} %param.17) | copy-start | bytes 393220
  353.6 3.4 copy-start.1
  363.0 3.4 copy-start.1
  372.4 3.4 copy-start.1
  381.8 3.4 copy-start.1
  391.1 3.4 copy-start.1
  400.5 3.4 copy-start.1
  409.9 3.4 copy-start.1
  419.3 3.4 copy-start.1
  428.6 3.4 copy-start.1
  438.0 3.4 copy-start.1
  447.4 3.4 copy-start.1
  456.7 3.4 copy-start.1
  466.1 3.4 copy-start.1
  475.5 3.4 copy-start.1
  484.9 3.4 copy-start.1
  494.2 3.4 copy-start.1
  519.6 77.1 %reduce-scatter.10.cloned.1.call-start = ((), (), s32[]{:S(2)}) async-start(), calls=%async_computation.6 | async-start | bytes 294912
Sparse Core Ops, SparseCore 0:
  33.5 116.5 reduce-scatter.7
  152.9 85.1 all-gather.2
  240.9 83.2 all-gather.4
  519.7 35.5 reduce-scatter.11
  557.7 39.0 reduce-scatter.9
where the time goes:
time: 608 us; the launch traced here: 605 us
  waiting for transfers between devices  312 us (51%)
  matrix products  97.6 us (16%)
  local copies, waits for them, and re-layouts  69 us (11%)
  other arithmetic  54.4 us (9%)
  blocking collectives  47.7 us (8%)
  between operations  13.4 us (2%)
  starting transfers between devices  9.7 us (2%)
    reduce_scatter x1, waiting for transfers between devices, per_device(): lax.psum_scatter(picked.reshape(slot_count * lax.axis_size('lat'), lon_ti...  114 us
    unnamed x7, waiting for transfers between devices  75.1 us
    dot_general x16, matrix products, absorb(): jnp.einsum('qhd,khd->qhk', queries, block_keys, preferred_element_type=jn...  60.8 us
    all_gather x1, waiting for transfers between devices, per_device(): lax.all_gather(values_local, 'lat', axis=0, tiled=True)  60.5 us
    all_gather x1, waiting for transfers between devices, per_device(): lax.all_gather(keys_local, 'lat', axis=0, tiled=True)  59 us
    reduce_sum x16, other arithmetic, absorb(): running_sum = running_sum * factor + jnp.sum(weights, axis=-1)  51.8 us
    dot_general x16, matrix products, absorb(): jnp.einsum('qhk,khd->qhd', weights.astype(jnp.bfloat16), block_values, pr...  33.2 us
    unnamed x20, local copies, waits for them, and re-layouts  31.6 us
  transfers between devices with their start and end apart: 8, of which 7 were waited for; matrix products, arithmetic and copies ran while one was open for 5% of the time, Pallas kernels for 0%

commit v1 on v0

--- a/solution.py
+++ b/solution.py
@@ -132,7 +132,9 @@
     )
     carry = sweep(
         initial,
-        lax.all_gather(keys_local, "lat", axis=0, tiled=True),
+        jnp.concatenate(
+            lax.all_to_all(jnp.stack([keys_local] * lax.axis_size("lat")), "lat", 0, 0), axis=0
+        ),
         lax.all_gather(values_local, "lat", axis=0, tiled=True),
         queries,
         band_total,

time: 608 us -> 532 us (0.88)
  waiting for transfers between devices: 312 us -> 223 us
  starting transfers between devices: 9.7 us -> 21.9 us
    all_gather x1 -> x0, waiting for transfers between devices: 59 us -> none  [per_device(): lax.all_gather(keys_local, 'lat', axis=0, tiled=True)]
    all_gather x1, waiting for transfers between devices: 60.5 us -> 32.8 us  [per_device(): lax.all_gather(values_local, 'lat', axis=0, tiled=True)]
    another operation x0 -> x2, local copies, waits for them, and re-layouts: none -> 15.4 us  [the longest x1 13 us: sweep(): keys_blocks = keys.reshape(blocks, block_len, H, head_size)]
    reshape x1 -> x0, local copies, waits for them, and re-layouts: 12.9 us -> none  [sweep(): keys_blocks = keys.reshape(blocks, block_len, H, head_size)]
    all_to_all x0 -> x1, starting transfers between devices: none -> 12.2 us  [per_device(): lax.all_to_all(jnp.stack([keys_local] * lax.axis_size('lat')), 'lat', 0, 0)]
    unnamed x7 -> x6, waiting for transfers between devices: 75.1 us -> 75.1 us
  transfers between devices with their start and end apart: 8 -> 8, of which waited for: 7 -> 6; matrix products, arithmetic and copies ran while one was open for 5% -> 6% of each run, Pallas kernels for 0% -> 0%
where the time goes in v1:
time: 532 us; the launch traced here: 530 us
  waiting for transfers between devices  223 us (42%)
  matrix products  96.8 us (18%)
  local copies, waits for them, and re-layouts  71.5 us (13%)
  other arithmetic  54.4 us (10%)
  blocking collectives  47.8 us (9%)
  starting transfers between devices  21.9 us (4%)
  between operations  13.4 us (3%)
    reduce_scatter x1, waiting for transfers between devices, per_device(): lax.psum_scatter(picked.reshape(slot_count * lax.axis_size('lat'), lon_ti...  112 us
    unnamed x6, waiting for transfers between devices  75.1 us
    dot_general x16, matrix products, absorb(): jnp.einsum('qhd,khd->qhk', queries, block_keys, preferred_element_type=jn...  60.6 us
    reduce_sum x16, other arithmetic, absorb(): running_sum = running_sum * factor + jnp.sum(weights, axis=-1)  51.8 us
    dot_general x16, matrix products, absorb(): jnp.einsum('qhk,khd->qhd', weights.astype(jnp.bfloat16), block_values, pr...  33.2 us
    all_gather x1, waiting for transfers between devices, per_device(): lax.all_gather(values_local, 'lat', axis=0, tiled=True)  32.8 us
    unnamed x20, local copies, waits for them, and re-layouts  31.6 us
    all_gather x1, blocking collectives, per_device(): gathered = lax.all_gather(mine, 'lon', axis=1, tiled=True)  28.9 us
  transfers between devices with their start and end apart: 8, of which 6 were waited for; matrix products, arithmetic and copies ran while one was open for 6% of the time, Pallas kernels for 0%

profile of v1, /device:TPU:32, one launch (start us, length us, event | category | flops | bytes accessed | tf_op | source)
XLA Modules:
  0.0 529.9 jit_solution(8567680295670568571)
XLA Ops:
  9.7 6.0 %collective-permute-start.1 = (bf16[73,2,128]{0,2,1:T(8,128)(2,1)S(1)}, bf16[73,2,128]{0,2,1:T(8,128)(2,1)S(1)}, u32[]{:S(2)}, u32[]{:S(2)}) collective-permute-start(bf16[73,2,128]{0,2,1:T(8,128)(2,1)S(1)} %get-tuple-element.120), channel_id=1, source_target_pairs={{8,0},{16,8},{24,16},{32,24},{40,32},{48,40},{56,48},{64,56},{72,6... | collective-permute-start | bytes 112136 | tf_op jit(solution)/shard_map/ppermute | solution.py:19
  36.1 12.2 %all-to-all-start = ((bf16[32,4,64,256]{3,2,1,0:T(8,128)(2,1)}), bf16[32,4,64,256]{3,2,1,0:T(8,128)(2,1)}, u32[]{:S(2)}, u32[]{:S(2)}) async-start(bf16[32,4,64,256]{3,2,1,0:T(8,128)(2,1)} %stack.19), calls=%async_computation | async-start | bytes 8388608 | tf_op jit(solution)/shard_map/all_to_all | solution.py:136
  49.6 112.0 %reduce-scatter.8.cloned.1.call-done = bf16[1,64,256]{2,1,0:T(8,128)(2,1)} async-done(((bf16[32,64,256]{2,1,0:T(8,128)(2,1)}), bf16[1,64,256]{2,1,0:T(8,128)(2,1)}) %reduce-scatter.8.cloned.1.call-update) | async-done | bytes 32784 | tf_op jit(solution)/shard_map/reduce_scatter | solution.py:109
  161.6 28.9 %all_gather.6 = bf16[1,512,256]{2,1,0:T(8,128)(2,1)S(1)} all-gather(bf16[1,64,256]{2,1,0:T(8,128)(2,1)} %reduce-scatter.8.cloned.1.call-done), channel_id=1, replica_groups=mesh['lat'=32,'lon'=8] {'lon'}, dimensions={1}, use_global_device_ids=true | all-gather | bytes 294912 | tf_op jit(solution)/shard_map/all_gather | solution.py:115
  190.7 13.0 %reshape_reshape.4 = bf16[16,512,4,64]{3,2,1,0:T(4,128)(2,1)} reshape(bf16[32,4,64,256]{3,2,1,0:T(8,128)(2,1)} %all-to-all-done) | data formatting | bytes 8388608 | tf_op jit(solution)/shard_map/reshape;reshape | solution.py:72
  203.6 12.7 %copy.27 = bf16[16,512,4,64]{1,3,2,0:T(8,128)(2,1)} copy(bf16[16,512,4,64]{3,2,1,0:T(4,128)(2,1)} %reshape_reshape.4) | data formatting | bytes 8388608
  216.4 32.8 %all-gather.2.cloned.1.call-done = bf16[128,64,256]{2,1,0:T(8,128)(2,1)} async-done(((bf16[4,64,256]{2,1,0:T(8,128)(2,1)}), bf16[128,64,256]{2,1,0:T(8,128)(2,1)}) %all-gather.2.cloned.1.call-update) | async-done | bytes 4194320 | tf_op jit(solution)/shard_map/all_gather | solution.py:138
  249.2 12.9 %reshape.107 = bf16[16,512,4,64]{3,2,1,0:T(4,128)(2,1)} reshape(bf16[128,64,256]{2,1,0:T(8,128)(2,1)} %all-gather.2.cloned.1.call-done) | data formatting | bytes 8388608 | tf_op jit(solution)/shard_map/reshape | solution.py:73
  262.1 12.7 %copy.28 = bf16[16,512,4,64]{1,3,2,0:T(8,128)(2,1)} copy(bf16[16,512,4,64]{3,2,1,0:T(4,128)(2,1)} %reshape.107) | data formatting | bytes 8388608
  274.9 149.8 %while.15 = (s32[]{:T(128)}, f32[512,4]{0,1:T(4,128)S(1)}, f32[512,4]{0,1:T(4,128)S(1)}, f32[512,4,64]{0,2,1:T(8,128)S(1)}, bf16[16,512,4,64]{1,3,2,0:T(8,128)(2...) while((s32[]{:T(128)}, f32[512,4]{0,1:T(4,128)S(1)}, ...), condition=%wide.region_5.6_spmd.clone, body=%wide.region_2.0_spmd.clone.sunk | while | flops 280373248 | bytes 31337616 | solution.py:82
  274.9 3.8 bitcast_reduce_fusion.2
  278.7 3.2 fusion.46
  284.3 3.8 bitcast_reduce_fusion.2
  288.1 3.2 fusion.46
  293.6 3.8 bitcast_reduce_fusion.2
  297.4 3.2 fusion.46
  303.0 3.8 bitcast_reduce_fusion.2
  312.3 3.8 bitcast_reduce_fusion.2
  321.7 3.8 bitcast_reduce_fusion.2
  331.1 3.8 bitcast_reduce_fusion.2
  340.4 3.8 bitcast_reduce_fusion.2
  349.8 3.8 bitcast_reduce_fusion.2
  359.1 3.8 bitcast_reduce_fusion.2
  368.5 3.8 bitcast_reduce_fusion.2
  377.9 3.8 bitcast_reduce_fusion.2
  387.2 3.8 bitcast_reduce_fusion.2
  396.6 3.8 bitcast_reduce_fusion.2
  405.9 3.8 bitcast_reduce_fusion.2
  415.3 3.8 bitcast_reduce_fusion.2
  424.6 18.9 %pmax.7 = f32[512,4]{0,1:T(4,128)S(1)} all-reduce(f32[512,4]{0,1:T(4,128)S(1)} %get-tuple-element.50), channel_id=1, replica_groups=mesh['lat'=32,'lon'=8] {'lon'}, use_global_device_ids=true, to_apply=%region_6.7 | all-reduce | flops 2048 | bytes 16384 | tf_op jit(solution)/shard_map/pmax | solution.py:143
  445.8 34.4 %reduce-scatter.12.cloned.1.call-done = bf16[64,4]{1,0:T(8,128)(2,1)} async-done(((bf16[512,4]{1,0:T(8,128)(2,1)}), bf16[64,4]{1,0:T(8,128)(2,1)}) %reduce-scatter.12.cloned.1.call-update) | async-done | bytes 528
  481.0 40.6 %reduce-scatter.10.cloned.1.call-done = bf16[64,256]{1,0:T(8,128)(2,1)} async-done(((bf16[512,256]{1,0:T(8,128)(2,1)}), bf16[64,256]{1,0:T(8,128)(2,1)}) %reduce-scatter.10.cloned.1.call-update) | async-done | bytes 32784
  (195 shorter events, 108.1 us)
Async XLA Ops:
  6.5 24.8 %copy-start = (bf16[256,256]{1,0:T(8,128)(2,1)S(1)}, bf16[256,256]{1,0:T(8,128)(2,1)}, u32[]{:S(2)}) copy-start(bf16[256,256]{1,0:T(8,128)(2,1)} %param.14) | copy-start | bytes 393220
  6.5 155.1 %reduce-scatter.8.cloned.1.call-start = ((), (), s32[]{:S(2)}) async-start(), calls=%async_computation.4 | async-start | bytes 1081344 | tf_op jit(solution)/shard_map/reduce_scatter | solution.py:109
  7.7 9.5 %collective-permute-start = (bf16[73,2,128]{0,2,1:T(8,128)(2,1)S(1)}, bf16[73,2,128]{0,2,1:T(8,128)(2,1)S(1)}, u32[]{:S(2)}, u32[]{:S(2)}) collective-permute-start(bf16[73,2,128]{0,2,1:T(8,128)(2,1)S(1)} %get-tuple-element.119), channel_id=1, source_target_pairs={{0,8},{8,16},{16,24},{24,32},{32,40},{40,48},{48,56},{56,64},{64,7... | collective-permute-start | bytes 112136 | tf_op jit(solution)/shard_map/ppermute | solution.py:18
  9.7 7.9 %collective-permute-start.1 = (bf16[73,2,128]{0,2,1:T(8,128)(2,1)S(1)}, bf16[73,2,128]{0,2,1:T(8,128)(2,1)S(1)}, u32[]{:S(2)}, u32[]{:S(2)}) collective-permute-start(bf16[73,2,128]{0,2,1:T(8,128)(2,1)S(1)} %get-tuple-element.120), channel_id=1, source_target_pairs={{8,0},{16,8},{24,16},{32,24},{40,32},{48,40},{56,48},{64,56},{72,6... | collective-permute-start | bytes 112136 | tf_op jit(solution)/shard_map/ppermute | solution.py:19
  17.6 5.8 %collective-permute-start.2 = (bf16[73,12,1]{0,2,1:T(2,128)(2,1)S(1)}, bf16[73,12,1]{0,2,1:T(2,128)(2,1)S(1)}, u32[]{:S(2)}, u32[]{:S(2)}) collective-permute-start(bf16[73,12,1]{0,2,1:T(2,128)(2,1)S(1)} %pad_maximum_fusion), channel_id=1, source_target_pairs={{0,1},{1,2},{2,3},{3,4},{4,5},{5,6},{6,7},{7,0},{8,9},{9,10},{10,1... | collective-permute-start | bytes 5264 | tf_op jit(solution)/shard_map/ppermute | solution.py:26
  29.7 3.6 copy-start.2
  36.1 12.3 %copy-start.3 = (bf16[256,256]{1,0:T(8,128)(2,1)S(1)}, bf16[256,256]{1,0:T(8,128)(2,1)}, u32[]{:S(2)}) copy-start(bf16[256,256]{1,0:T(8,128)(2,1)} %param.16) | copy-start | bytes 393220
  36.1 154.6 %all-to-all-start = ((bf16[32,4,64,256]{3,2,1,0:T(8,128)(2,1)}), bf16[32,4,64,256]{3,2,1,0:T(8,128)(2,1)}, u32[]{:S(2)}, u32[]{:S(2)}) async-start(bf16[32,4,64,256]{3,2,1,0:T(8,128)(2,1)} %stack.19), calls=%async_computation | async-start | bytes 8388608 | tf_op jit(solution)/shard_map/all_to_all | solution.py:136
  48.3 200.9 %all-gather.2.cloned.1.call-start = ((), (), s32[]{:S(2)}) async-start(), calls=%async_computation.5 | async-start | bytes 4325376 | tf_op jit(solution)/shard_map/all_gather | solution.py:138
  49.3 430.9 %reduce-scatter.12.cloned.1.call-start = ((), (), s32[]{:S(2)}) async-start(), calls=%async_computation.7 | async-start | bytes 147456
  274.9 247.7 %copy-start.4 = (bf16[256,256]{1,0:T(8,128)(2,1)S(1)}, bf16[256,256]{1,0:T(8,128)(2,1)}, u32[]{:S(2)}) copy-start(bf16[256,256]{1,0:T(8,128)(2,1)} %param.17) | copy-start | bytes 393220
  278.7 3.4 copy-start.1
  288.0 3.4 copy-start.1
  297.4 3.4 copy-start.1
  306.8 3.4 copy-start.1
  316.1 3.4 copy-start.1
  325.5 3.4 copy-start.1
  334.8 3.4 copy-start.1
  344.2 3.4 copy-start.1
  353.6 3.4 copy-start.1
  362.9 3.4 copy-start.1
  372.3 3.4 copy-start.1
  381.7 3.4 copy-start.1
  391.0 3.4 copy-start.1
  400.4 3.4 copy-start.1
  409.7 3.4 copy-start.1
  419.1 3.4 copy-start.1
  444.5 77.1 %reduce-scatter.10.cloned.1.call-start = ((), (), s32[]{:S(2)}) async-start(), calls=%async_computation.6 | async-start | bytes 294912
Sparse Core Ops, SparseCore 0:
  33.5 128.0 reduce-scatter.7
  164.4 84.7 all-gather.1
  444.6 35.5 reduce-scatter.11
  482.5 39.0 reduce-scatter.9
